TPU v7x, 32 devices: a whole 2x2x4 slice. The times are simulated.
32 devices in a mesh: mem: 4 (over z), space: 8 (over y, x, core).
Axes of the slice: x: 2, y: 2, z: 4, core: 2. Of those that a mesh axis runs over, the one named last changes fastest.
Arguments:
- ensemble: float32 [128, 16, 2048], P('mem', 'space'), may hold values from -6 to 6
- forcing: float32 [16, 2048], P('space'), may hold values from 2 to 8
- obs_cell: int32 [1024], P('space'), may hold values from 0 to 32767, as said below
- obs_value: float32 [1024], P('space'), may hold values from -8 to 8
- obs_var: float32 [1024], P('space'), may hold values from 0.5 to 2
- obs_noise: float32 [128, 1024], P('mem', 'space'), may hold values from -5 to 5
Outputs:
- analysis: float32 [128, 16, 2048], P('mem', 'space')
Inputs may be any that keep to these rules, and one draw needn't show every extreme that they name: `obs_cell`: entries 128 * s to 128 * (s + 1) - 1 name cells of planes 2 * s to 2 * (s + 1) - 1, a cell of plane x and position p having index x * 2048 + p.
All inputs are finite; a program needn't handle non-finite values.
Results may differ from a plain program's by a relative error of at most 0.00018.
Values sent between devices are 32-bit elements; how exact they have to be, the bound alone decides.
No kernel may reach another device: no remote copies, remote signals or barrier semaphores. Data moves between devices by JAX's collectives and lax.ppermute only.
A program may use at most 64 MiB of HBM per device.

v0:
```python
import jax
import jax.numpy as jnp
from jax import lax
from jax.sharding import PartitionSpec as P

FSTEPS = 4
ITERS = 6
time_step = 0.05
highest = lax.Precision.HIGHEST


def from_behind(value, axis, steps):
    count = lax.axis_size(axis)
    pairs = [(source, (source + steps) % count) for source in range(count)]
    return lax.ppermute(value, axis, pairs)


def padded_2(x, sides, width):
    for axis, dim in sides:
        size, length = (lax.axis_size(axis), x.shape[dim])
        up = [(i, (i + 1) % size) for i in range(size)]
        down = [(j, i) for i, j in up]
        last = lax.slice_in_dim(x, length - width, length, axis=dim)
        initial = lax.slice_in_dim(x, 0, width, axis=dim)
        before = lax.ppermute(last, axis, up)
        after = lax.ppermute(initial, axis, down)
        x = jnp.concatenate([before, x, after], axis=dim)
    return x


def taper_of(planes_a, planes_b, planes_all, reach_planes):
    spread = jnp.abs(planes_a[:, None] - planes_b[None, :])
    spread = jnp.minimum(spread, planes_all - spread)
    return jnp.maximum(0.0, 1.0 - spread.astype(jnp.float32) / reach_planes)


def collect_band(values, along, reach_slabs, mover):
    pieces = []
    for offset in range(-reach_slabs, reach_slabs + 1):
        if offset == 0:
            pieces.append(values)
        else:
            pieces.append(mover(values, -offset))
    return jnp.concatenate(pieces, axis=along)


def move_obs(values, amount):
    return from_behind(values, "space", amount)


def move_directions(values, amount):
    return from_behind(values, "space", amount)


def move_weights(values, amount):
    return from_behind(values, "space", amount)


def shards(ensemble, forcing, obs_cell, obs_value, obs_var, obs_noise):
    members_dev, planes_dev, plane_cells = ensemble.shape
    obs_dev = obs_cell.shape[0]
    space_count = lax.axis_size("space")
    mem_count = lax.axis_size("mem")
    space_index = lax.axis_index("space")
    mem_index = lax.axis_index("mem")
    members = members_dev * mem_count
    planes_all = planes_dev * space_count
    reach_slabs = min(8, space_count // 4)
    reach_planes = planes_dev * reach_slabs
    band_width = reach_slabs * obs_dev
    states = ensemble
    for counter in range(FSTEPS):
        padded = padded_2(states, (("space", 1),), 2)
        forward_one = padded[:, 3 : 3 + planes_dev]
        back_one = padded[:, 1 : 1 + planes_dev]
        back_two = padded[:, 0:planes_dev]
        states = states + time_step * ((forward_one - back_two) * back_one - states + forcing)
    slab_cells = planes_dev * plane_cells
    local_cells = obs_cell - space_index * slab_cells
    observed = jnp.take(states.reshape(members_dev, slab_cells), local_cells, axis=1)
    own_planes = obs_cell // plane_cells
    own_rows = lax.all_gather(observed, "mem", axis=0, tiled=True)
    own_mean = jnp.sum(own_rows, axis=0) / members
    own_anom = own_rows - own_mean
    stacked = jnp.concatenate([own_anom, own_planes.astype(jnp.float32)[None, :]], axis=0)
    band = collect_band(stacked, 1, reach_slabs, move_obs)
    context_anom = band[:members]
    context_planes = band[members].astype(jnp.int32)
    context_count = context_anom.shape[1]
    taper_block = taper_of(own_planes, context_planes, planes_all, reach_planes)
    gram_block = jnp.dot(own_anom.T, context_anom, precision=highest) / (members - 1)
    diagonal = jnp.arange(context_count)[None, :] == (band_width + jnp.arange(obs_dev))[:, None]
    covariance = taper_block * gram_block + jnp.where(diagonal, obs_var[:, None], 0.0)
    row_max = jnp.max(jnp.sum(jnp.abs(covariance), axis=1))
    var_min = jnp.min(obs_var)
    both = lax.pmax((row_max, -var_min), "space")
    upper_bound = both[0]
    lower_bound = -both[1]
    mean_rhs = obs_value - own_mean
    member_anom = lax.dynamic_slice_in_dim(own_anom, mem_index * members_dev, members_dev, 0)
    anom_rhs = (jnp.sqrt(obs_var)[None, :] * obs_noise - member_anom).T
    center = (upper_bound + lower_bound) / 2.0
    radius = (upper_bound - lower_bound) / 2.0
    sigma_ratio = center / radius
    rho_now = 1.0 / sigma_ratio
    resid_anom, resid_mean = (anom_rhs, mean_rhs)
    dir_anom, dir_mean = (anom_rhs / center, mean_rhs / center)
    anom_weight = jnp.zeros_like(anom_rhs)
    mean_weight = jnp.zeros_like(mean_rhs)
    for iteration in range(ITERS):
        anom_weight = anom_weight + dir_anom
        mean_weight = mean_weight + dir_mean
        if iteration < ITERS - 1:
            joined = jnp.concatenate([dir_anom, dir_mean[:, None]], axis=1)
            band_dirs = collect_band(joined, 0, reach_slabs, move_directions)
            image = jnp.dot(covariance, band_dirs, precision=highest)
            image_anom = image[:, :-1]
            image_mean = image[:, -1]
            resid_anom = resid_anom - image_anom
            resid_mean = resid_mean - image_mean
            rho_next = 1.0 / (2.0 * sigma_ratio - rho_now)
            dir_anom = rho_next * rho_now * dir_anom + 2.0 * rho_next / radius * resid_anom
            dir_mean = rho_next * rho_now * dir_mean + 2.0 * rho_next / radius * resid_mean
            rho_now = rho_next
    weight = anom_weight + mean_weight[:, None]
    owned_cells = lax.all_to_all(states, "mem", split_axis=2, concat_axis=0, tiled=True)
    weight_rows = lax.all_gather(weight, "mem", axis=1, tiled=True)
    weight_context = collect_band(weight_rows, 0, reach_slabs, move_weights)
    own_plane_ids = space_index * planes_dev + jnp.arange(planes_dev, dtype=jnp.int32)
    plane_taper = taper_of(own_plane_ids, context_planes, planes_all, reach_planes)

    def plane_gain(taper_row):
        return jnp.dot(context_anom * taper_row[None, :], weight_context, precision=highest)

    gain_blocks = lax.map(plane_gain, plane_taper)
    state_mean = jnp.sum(owned_cells, axis=0) / members
    state_anom = owned_cells - state_mean
    update = jnp.einsum("jxp,xjk->kxp", state_anom, gain_blocks, precision=highest) / (members - 1)
    analysis = owned_cells + update
    return lax.all_to_all(analysis, "mem", split_axis=0, concat_axis=2, tiled=True)


def solution(mesh):
    placed = (
        P("mem", "space", None),
        P("space", None),
        P("space"),
        P("space"),
        P("space"),
        P("mem", "space"),
    )
    return jax.shard_map(
        shards, mesh=mesh, in_specs=placed, out_specs=P("mem", "space", None), check_vma=False
    )
```

profile of v0, /device:TPU:6, one launch (start us, length us, event | category | flops | bytes accessed | tf_op | source)
XLA Modules:
  0.0 197.6 jit_solution(11910632786536468640)
XLA Ops:
  1.9 10.0 %collective-permute-done = f32[32,2,2048]{2,0,1:T(8,128)S(1)} collective-permute-done((f32[32,2,2048]{2,0,1:T(8,128)S(1)}, f32[32,2,2048]{2,0,1:T(8,128)S(1)}, u32[]{:S(2)}, u32[]{:S(2)}) %collective-permute-start) | collective-permute-done | bytes 524320 | tf_op jit(solution)/shard_map/ppermute | solution.py:26
  12.0 3.6 %collective-permute-done.1 = f32[32,2,2048]{2,0,1:T(8,128)S(1)} collective-permute-done((f32[32,2,2048]{2,0,1:T(8,128)S(1)}, f32[32,2,2048]{2,0,1:T(8,128)S(1)}, u32[]{:S(2)}, u32[]{:S(2)}) %collective-permute-start.1) | collective-permute-done | bytes 524320 | tf_op jit(solution)/shard_map/ppermute | solution.py:25
  18.3 10.7 %collective-permute-done.3 = f32[32,2,2048]{2,0,1:T(8,128)S(1)} collective-permute-done((f32[32,2,2048]{2,0,1:T(8,128)S(1)}, f32[32,2,2048]{2,0,1:T(8,128)S(1)}, u32[]{:S(2)}, u32[]{:S(2)}) %collective-permute-start.3) | collective-permute-done | bytes 524320 | tf_op jit(solution)/shard_map/ppermute | solution.py:25
  33.4 7.9 %collective-permute-done.5 = f32[32,2,2048]{2,0,1:T(8,128)S(1)} collective-permute-done((f32[32,2,2048]{2,0,1:T(8,128)S(1)}, f32[32,2,2048]{2,0,1:T(8,128)S(1)}, u32[]{:S(2)}, u32[]{:S(2)}) %collective-permute-start.5) | collective-permute-done | bytes 524320 | tf_op jit(solution)/shard_map/ppermute | solution.py:25
  41.4 2.9 %collective-permute-done.4 = f32[32,2,2048]{2,0,1:T(8,128)S(1)} collective-permute-done((f32[32,2,2048]{2,0,1:T(8,128)S(1)}, f32[32,2,2048]{2,0,1:T(8,128)S(1)}, u32[]{:S(2)}, u32[]{:S(2)}) %collective-permute-start.4) | collective-permute-done | bytes 524320 | tf_op jit(solution)/shard_map/ppermute | solution.py:26
  46.8 9.0 %collective-permute-done.7 = f32[32,2,2048]{2,0,1:T(8,128)S(1)} collective-permute-done((f32[32,2,2048]{2,0,1:T(8,128)S(1)}, f32[32,2,2048]{2,0,1:T(8,128)S(1)}, u32[]{:S(2)}, u32[]{:S(2)}) %collective-permute-start.7) | collective-permute-done | bytes 524320 | tf_op jit(solution)/shard_map/ppermute | solution.py:25
  55.7 3.0 %collective-permute-done.6 = f32[32,2,2048]{2,0,1:T(8,128)S(1)} collective-permute-done((f32[32,2,2048]{2,0,1:T(8,128)S(1)}, f32[32,2,2048]{2,0,1:T(8,128)S(1)}, u32[]{:S(2)}, u32[]{:S(2)}) %collective-permute-start.6) | collective-permute-done | bytes 524320 | tf_op jit(solution)/shard_map/ppermute | solution.py:26
  60.1 13.4 %all_gather.6 = f32[128,128]{1,0:T(8,128)S(1)} all-gather(f32[32,128]{1,0:T(8,128)S(1)} %select_bitcast_fusion), channel_id=1, replica_groups=mesh['mem'=4,'space'=8] {'mem'}, dimensions={0}, use_global_device_ids=true | all-gather | bytes 81920 | tf_op jit(solution)/shard_map/all_gather | solution.py:82
  73.6 3.9 %collective-permute-start.8 = (f32[129,128]{1,0:T(8,128)S(1)}, f32[129,128]{1,0:T(8,128)S(1)}, u32[]{:S(2)}, u32[]{:S(2)}) collective-permute-start(f32[129,128]{1,0:T(8,128)S(1)} %pad_maximum_fusion.8), channel_id=1, source_target_pairs={{0,2},{1,3},{2,4},{3,5},{4,6},{5,7},{6,0},{7,1},{8,10},{9,11},{10,... | collective-permute-start | bytes 198152 | tf_op jit(solution)/shard_map/ppermute | solution.py:15
  79.4 2.5 %collective-permute-done.9 = f32[129,128]{1,0:T(8,128)S(1)} collective-permute-done((f32[129,128]{1,0:T(8,128)S(1)}, f32[129,128]{1,0:T(8,128)S(1)}, u32[]{:S(2)}, u32[]{:S(2)}) %collective-permute-start.9) | collective-permute-done | bytes 66080 | tf_op jit(solution)/shard_map/ppermute | solution.py:15
  84.6 11.5 %all-reduce = (f32[]{:T(128)}, f32[]{:T(128)}) all-reduce(f32[]{:T(128)} %reduce_max.9, f32[]{:T(128)S(6)} %neg.6), channel_id=1, replica_groups=mesh['mem'=4,'space'=8] {'space'}, use_global_device_ids=true, to_apply=%region_3.4 | all-reduce | flops 2 | bytes 16 | tf_op jit(solution)/shard_map/pmax | solution.py:96
  97.4 4.1 %collective-permute-start.12 = (f32[128,33]{0,1:T(8,128)S(1)}, f32[128,33]{0,1:T(8,128)S(1)}, u32[]{:S(2)}, u32[]{:S(2)}) collective-permute-start(f32[128,33]{0,1:T(8,128)S(1)} %pad_maximum_fusion.9), channel_id=1, source_target_pairs={{0,2},{1,3},{2,4},{3,5},{4,6},{5,7},{6,0},{7,1},{8,10},{9,11},{10,... | collective-permute-start | bytes 50696 | tf_op jit(solution)/shard_map/ppermute | solution.py:15
  102.9 2.8 %collective-permute-done.13 = f32[128,33]{0,1:T(8,128)S(1)} collective-permute-done((f32[128,33]{0,1:T(8,128)S(1)}, f32[128,33]{0,1:T(8,128)S(1)}, u32[]{:S(2)}, u32[]{:S(2)}) %collective-permute-start.13) | collective-permute-done | bytes 16928 | tf_op jit(solution)/shard_map/ppermute | solution.py:15
  107.6 2.4 %collective-permute-start.16 = (f32[128,33]{0,1:T(8,128)S(1)}, f32[128,33]{0,1:T(8,128)S(1)}, u32[]{:S(2)}, u32[]{:S(2)}) collective-permute-start(f32[128,33]{0,1:T(8,128)S(1)} %pad_maximum_fusion.10), channel_id=1, source_target_pairs={{0,2},{1,3},{2,4},{3,5},{4,6},{5,7},{6,0},{7,1},{8,10},{9,11},{10,... | collective-permute-start | bytes 50696 | tf_op jit(solution)/shard_map/ppermute | solution.py:15
  115.4 2.4 %collective-permute-start.20 = (f32[128,33]{0,1:T(8,128)S(1)}, f32[128,33]{0,1:T(8,128)S(1)}, u32[]{:S(2)}, u32[]{:S(2)}) collective-permute-start(f32[128,33]{0,1:T(8,128)S(1)} %pad_maximum_fusion.11), channel_id=1, source_target_pairs={{0,2},{1,3},{2,4},{3,5},{4,6},{5,7},{6,0},{7,1},{8,10},{9,11},{10,... | collective-permute-start | bytes 50696 | tf_op jit(solution)/shard_map/ppermute | solution.py:15
  123.3 2.4 %collective-permute-start.24 = (f32[128,33]{0,1:T(8,128)S(1)}, f32[128,33]{0,1:T(8,128)S(1)}, u32[]{:S(2)}, u32[]{:S(2)}) collective-permute-start(f32[128,33]{0,1:T(8,128)S(1)} %pad_maximum_fusion.12), channel_id=1, source_target_pairs={{0,2},{1,3},{2,4},{3,5},{4,6},{5,7},{6,0},{7,1},{8,10},{9,11},{10,... | collective-permute-start | bytes 50696 | tf_op jit(solution)/shard_map/ppermute | solution.py:15
  131.1 2.4 %collective-permute-start.28 = (f32[128,33]{0,1:T(8,128)S(1)}, f32[128,33]{0,1:T(8,128)S(1)}, u32[]{:S(2)}, u32[]{:S(2)}) collective-permute-start(f32[128,33]{0,1:T(8,128)S(1)} %pad_maximum_fusion.13), channel_id=1, source_target_pairs={{0,2},{1,3},{2,4},{3,5},{4,6},{5,7},{6,0},{7,1},{8,10},{9,11},{10,... | collective-permute-start | bytes 50696 | tf_op jit(solution)/shard_map/ppermute | solution.py:15
  134.6 2.9 %reshape.39 = f32[4,1,32768]{2,1,0:T(1,128)} reshape(f32[2048,2,32]{2,1,0:T(2,128)S(1)} %bitcast.106) | data formatting | bytes 1048576
  137.5 4.7 %all-to-all-start = ((f32[4,1,32768]{2,1,0:T(1,128)}), f32[4,1,32768]{2,1,0:T(1,128)S(1)}, u32[]{:S(2)}, u32[]{:S(2)}) async-start(f32[4,1,32768]{2,1,0:T(1,128)} %reshape.39), calls=%async_computation | async-start | bytes 1048576 | tf_op jit(solution)/shard_map/all_to_all | solution.py:126
  142.8 2.9 %collective-permute-done.29 = f32[128,33]{0,1:T(8,128)S(1)} collective-permute-done((f32[128,33]{0,1:T(8,128)S(1)}, f32[128,33]{0,1:T(8,128)S(1)}, u32[]{:S(2)}, u32[]{:S(2)}) %collective-permute-start.29) | collective-permute-done | bytes 16928 | tf_op jit(solution)/shard_map/ppermute | solution.py:15
  147.5 13.8 %all_gather.7 = f32[128,128]{0,1:T(8,128)S(1)} all-gather(f32[128,32]{0,1:T(8,128)S(1)} %fusion.38), channel_id=1, replica_groups=mesh['mem'=4,'space'=8] {'mem'}, dimensions={1}, use_global_device_ids=true | all-gather | bytes 81920 | tf_op jit(solution)/shard_map/all_gather | solution.py:127
  161.3 2.3 %collective-permute-start.32 = (f32[128,128]{0,1:T(8,128)S(1)}, f32[128,128]{0,1:T(8,128)S(1)}, u32[]{:S(2)}, u32[]{:S(2)}) collective-permute-start(f32[128,128]{0,1:T(8,128)S(1)} %all_gather.7), channel_id=1, source_target_pairs={{0,2},{1,3},{2,4},{3,5},{4,6},{5,7},{6,0},{7,1},{8,10},{9,11},{10,... | collective-permute-start | bytes 196616 | tf_op jit(solution)/shard_map/ppermute | solution.py:15
  165.6 2.8 %collective-permute-done.33 = f32[128,128]{0,1:T(8,128)S(1)} collective-permute-done((f32[128,128]{0,1:T(8,128)S(1)}, f32[128,128]{0,1:T(8,128)S(1)}, u32[]{:S(2)}, u32[]{:S(2)}) %collective-permute-start.33) | collective-permute-done | bytes 65568 | tf_op jit(solution)/shard_map/ppermute | solution.py:15
  177.2 19.5 %all_to_all.36 = f32[128,2,512]{2,1,0:T(2,128)S(1)} all-to-all(f32[128,2,512]{2,1,0:T(2,128)S(1)} %copy.43), channel_id=1, replica_groups=mesh['mem'=4,'space'=8] {'mem'}, dimensions={0} | all-to-all | bytes 1048576 | tf_op jit(solution)/shard_map/all_to_all | solution.py:140
  (166 shorter events, 51.0 us)
Async XLA Ops:
  1.4 10.6 %collective-permute-start = (f32[32,2,2048]{2,0,1:T(8,128)S(1)}, f32[32,2,2048]{2,0,1:T(8,128)S(1)}, u32[]{:S(2)}, u32[]{:S(2)}) collective-permute-start(f32[32,2,2048]{2,0,1:T(8,128)S(1)} %copy.36), channel_id=1, source_target_pairs={{1,0},{2,1},{3,2},{4,3},{5,4},{6,5},{7,6},{0,7},{9,8},{10,9},{11,1... | collective-permute-start | bytes 1572872 | tf_op jit(solution)/shard_map/ppermute | solution.py:26
  1.4 14.2 %collective-permute-start.1 = (f32[32,2,2048]{2,0,1:T(8,128)S(1)}, f32[32,2,2048]{2,0,1:T(8,128)S(1)}, u32[]{:S(2)}, u32[]{:S(2)}) collective-permute-start(f32[32,2,2048]{2,0,1:T(8,128)S(1)} %copy.36), channel_id=1, source_target_pairs={{0,1},{1,2},{2,3},{3,4},{4,5},{5,6},{6,7},{7,0},{8,9},{9,10},{10,1... | collective-permute-start | bytes 1572872 | tf_op jit(solution)/shard_map/ppermute | solution.py:25
  16.5 12.5 %collective-permute-start.3 = (f32[32,2,2048]{2,0,1:T(8,128)S(1)}, f32[32,2,2048]{2,0,1:T(8,128)S(1)}, u32[]{:S(2)}, u32[]{:S(2)}) collective-permute-start(f32[32,2,2048]{2,0,1:T(8,128)S(1)} %fusion.29), channel_id=1, source_target_pairs={{0,1},{1,2},{2,3},{3,4},{4,5},{5,6},{6,7},{7,0},{8,9},{9,10},{10,1... | collective-permute-start | bytes 1572872 | tf_op jit(solution)/shard_map/ppermute | solution.py:25
  16.5 13.3 %collective-permute-start.2 = (f32[32,2,2048]{2,0,1:T(8,128)S(1)}, f32[32,2,2048]{2,0,1:T(8,128)S(1)}, u32[]{:S(2)}, u32[]{:S(2)}) collective-permute-start(f32[32,2,2048]{2,0,1:T(8,128)S(1)} %fusion.29), channel_id=1, source_target_pairs={{1,0},{2,1},{3,2},{4,3},{5,4},{6,5},{7,6},{0,7},{9,8},{10,9},{11,1... | collective-permute-start | bytes 1572872 | tf_op jit(solution)/shard_map/ppermute | solution.py:26
  29.9 11.5 %collective-permute-start.5 = (f32[32,2,2048]{2,0,1:T(8,128)S(1)}, f32[32,2,2048]{2,0,1:T(8,128)S(1)}, u32[]{:S(2)}, u32[]{:S(2)}) collective-permute-start(f32[32,2,2048]{2,0,1:T(8,128)S(1)} %fusion.23), channel_id=1, source_target_pairs={{0,1},{1,2},{2,3},{3,4},{4,5},{5,6},{6,7},{7,0},{8,9},{9,10},{10,1... | collective-permute-start | bytes 1572872 | tf_op jit(solution)/shard_map/ppermute | solution.py:25
  30.0 14.3 %collective-permute-start.4 = (f32[32,2,2048]{2,0,1:T(8,128)S(1)}, f32[32,2,2048]{2,0,1:T(8,128)S(1)}, u32[]{:S(2)}, u32[]{:S(2)}) collective-permute-start(f32[32,2,2048]{2,0,1:T(8,128)S(1)} %fusion.23), channel_id=1, source_target_pairs={{1,0},{2,1},{3,2},{4,3},{5,4},{6,5},{7,6},{0,7},{9,8},{10,9},{11,1... | collective-permute-start | bytes 1572872 | tf_op jit(solution)/shard_map/ppermute | solution.py:26
  44.4 11.3 %collective-permute-start.7 = (f32[32,2,2048]{2,0,1:T(8,128)S(1)}, f32[32,2,2048]{2,0,1:T(8,128)S(1)}, u32[]{:S(2)}, u32[]{:S(2)}) collective-permute-start(f32[32,2,2048]{2,0,1:T(8,128)S(1)} %fusion.17), channel_id=1, source_target_pairs={{0,1},{1,2},{2,3},{3,4},{4,5},{5,6},{6,7},{7,0},{8,9},{9,10},{10,1... | collective-permute-start | bytes 1572872 | tf_op jit(solution)/shard_map/ppermute | solution.py:25
  44.6 14.1 %collective-permute-start.6 = (f32[32,2,2048]{2,0,1:T(8,128)S(1)}, f32[32,2,2048]{2,0,1:T(8,128)S(1)}, u32[]{:S(2)}, u32[]{:S(2)}) collective-permute-start(f32[32,2,2048]{2,0,1:T(8,128)S(1)} %fusion.17), channel_id=1, source_target_pairs={{1,0},{2,1},{3,2},{4,3},{5,4},{6,5},{7,6},{0,7},{9,8},{10,9},{11,1... | collective-permute-start | bytes 1572872 | tf_op jit(solution)/shard_map/ppermute | solution.py:26
  73.6 5.9 %collective-permute-start.8 = (f32[129,128]{1,0:T(8,128)S(1)}, f32[129,128]{1,0:T(8,128)S(1)}, u32[]{:S(2)}, u32[]{:S(2)}) collective-permute-start(f32[129,128]{1,0:T(8,128)S(1)} %pad_maximum_fusion.8), channel_id=1, source_target_pairs={{0,2},{1,3},{2,4},{3,5},{4,6},{5,7},{6,0},{7,1},{8,10},{9,11},{10,... | collective-permute-start | bytes 198152 | tf_op jit(solution)/shard_map/ppermute | solution.py:15
  77.5 5.8 %collective-permute-start.11 = (f32[129,128]{1,0:T(8,128)S(1)}, f32[129,128]{1,0:T(8,128)S(1)}, u32[]{:S(2)}, u32[]{:S(2)}) collective-permute-start(f32[129,128]{1,0:T(8,128)S(1)} %pad_maximum_fusion.8), channel_id=1, source_target_pairs={{0,6},{1,7},{2,0},{3,1},{4,2},{5,3},{6,4},{7,5},{8,14},{9,15},{10,... | collective-permute-start | bytes 198152 | tf_op jit(solution)/shard_map/ppermute | solution.py:15
  77.5 4.4 %collective-permute-start.10 = (f32[129,128]{1,0:T(8,128)S(1)}, f32[129,128]{1,0:T(8,128)S(1)}, u32[]{:S(2)}, u32[]{:S(2)}) collective-permute-start(f32[129,128]{1,0:T(8,128)S(1)} %pad_maximum_fusion.8), channel_id=1, source_target_pairs={{0,7},{1,0},{2,1},{3,2},{4,3},{5,4},{6,5},{7,6},{8,15},{9,8},{10,9... | collective-permute-start | bytes 198152 | tf_op jit(solution)/shard_map/ppermute | solution.py:15
  77.5 4.4 %collective-permute-start.9 = (f32[129,128]{1,0:T(8,128)S(1)}, f32[129,128]{1,0:T(8,128)S(1)}, u32[]{:S(2)}, u32[]{:S(2)}) collective-permute-start(f32[129,128]{1,0:T(8,128)S(1)} %pad_maximum_fusion.8), channel_id=1, source_target_pairs={{0,1},{1,2},{2,3},{3,4},{4,5},{5,6},{6,7},{7,0},{8,9},{9,10},{10,1... | collective-permute-start | bytes 198152 | tf_op jit(solution)/shard_map/ppermute | solution.py:15
  97.4 5.6 %collective-permute-start.12 = (f32[128,33]{0,1:T(8,128)S(1)}, f32[128,33]{0,1:T(8,128)S(1)}, u32[]{:S(2)}, u32[]{:S(2)}) collective-permute-start(f32[128,33]{0,1:T(8,128)S(1)} %pad_maximum_fusion.9), channel_id=1, source_target_pairs={{0,2},{1,3},{2,4},{3,5},{4,6},{5,7},{6,0},{7,1},{8,10},{9,11},{10,... | collective-permute-start | bytes 50696 | tf_op jit(solution)/shard_map/ppermute | solution.py:15
  102.2 4.8 %collective-permute-start.15 = (f32[128,33]{0,1:T(8,128)S(1)}, f32[128,33]{0,1:T(8,128)S(1)}, u32[]{:S(2)}, u32[]{:S(2)}) collective-permute-start(f32[128,33]{0,1:T(8,128)S(1)} %pad_maximum_fusion.9), channel_id=1, source_target_pairs={{0,6},{1,7},{2,0},{3,1},{4,2},{5,3},{6,4},{7,5},{8,14},{9,15},{10,... | collective-permute-start | bytes 50696 | tf_op jit(solution)/shard_map/ppermute | solution.py:15
  110.1 4.8 %collective-permute-start.19 = (f32[128,33]{0,1:T(8,128)S(1)}, f32[128,33]{0,1:T(8,128)S(1)}, u32[]{:S(2)}, u32[]{:S(2)}) collective-permute-start(f32[128,33]{0,1:T(8,128)S(1)} %pad_maximum_fusion.10), channel_id=1, source_target_pairs={{0,6},{1,7},{2,0},{3,1},{4,2},{5,3},{6,4},{7,5},{8,14},{9,15},{10,... | collective-permute-start | bytes 50696 | tf_op jit(solution)/shard_map/ppermute | solution.py:15
  117.9 4.8 %collective-permute-start.23 = (f32[128,33]{0,1:T(8,128)S(1)}, f32[128,33]{0,1:T(8,128)S(1)}, u32[]{:S(2)}, u32[]{:S(2)}) collective-permute-start(f32[128,33]{0,1:T(8,128)S(1)} %pad_maximum_fusion.11), channel_id=1, source_target_pairs={{0,6},{1,7},{2,0},{3,1},{4,2},{5,3},{6,4},{7,5},{8,14},{9,15},{10,... | collective-permute-start | bytes 50696 | tf_op jit(solution)/shard_map/ppermute | solution.py:15
  125.8 4.8 %collective-permute-start.27 = (f32[128,33]{0,1:T(8,128)S(1)}, f32[128,33]{0,1:T(8,128)S(1)}, u32[]{:S(2)}, u32[]{:S(2)}) collective-permute-start(f32[128,33]{0,1:T(8,128)S(1)} %pad_maximum_fusion.12), channel_id=1, source_target_pairs={{0,6},{1,7},{2,0},{3,1},{4,2},{5,3},{6,4},{7,5},{8,14},{9,15},{10,... | collective-permute-start | bytes 50696 | tf_op jit(solution)/shard_map/ppermute | solution.py:15
  131.1 11.7 %collective-permute-start.28 = (f32[128,33]{0,1:T(8,128)S(1)}, f32[128,33]{0,1:T(8,128)S(1)}, u32[]{:S(2)}, u32[]{:S(2)}) collective-permute-start(f32[128,33]{0,1:T(8,128)S(1)} %pad_maximum_fusion.13), channel_id=1, source_target_pairs={{0,2},{1,3},{2,4},{3,5},{4,6},{5,7},{6,0},{7,1},{8,10},{9,11},{10,... | collective-permute-start | bytes 50696 | tf_op jit(solution)/shard_map/ppermute | solution.py:15
  137.5 33.2 %all-to-all-start = ((f32[4,1,32768]{2,1,0:T(1,128)}), f32[4,1,32768]{2,1,0:T(1,128)S(1)}, u32[]{:S(2)}, u32[]{:S(2)}) async-start(f32[4,1,32768]{2,1,0:T(1,128)} %reshape.39), calls=%async_computation | async-start | bytes 1048576 | tf_op jit(solution)/shard_map/all_to_all | solution.py:126
  142.2 4.8 %collective-permute-start.31 = (f32[128,33]{0,1:T(8,128)S(1)}, f32[128,33]{0,1:T(8,128)S(1)}, u32[]{:S(2)}, u32[]{:S(2)}) collective-permute-start(f32[128,33]{0,1:T(8,128)S(1)} %pad_maximum_fusion.13), channel_id=1, source_target_pairs={{0,6},{1,7},{2,0},{3,1},{4,2},{5,3},{6,4},{7,5},{8,14},{9,15},{10,... | collective-permute-start | bytes 50696 | tf_op jit(solution)/shard_map/ppermute | solution.py:15
  161.3 4.3 %collective-permute-start.32 = (f32[128,128]{0,1:T(8,128)S(1)}, f32[128,128]{0,1:T(8,128)S(1)}, u32[]{:S(2)}, u32[]{:S(2)}) collective-permute-start(f32[128,128]{0,1:T(8,128)S(1)} %all_gather.7), channel_id=1, source_target_pairs={{0,2},{1,3},{2,4},{3,5},{4,6},{5,7},{6,0},{7,1},{8,10},{9,11},{10,... | collective-permute-start | bytes 196616 | tf_op jit(solution)/shard_map/ppermute | solution.py:15
  163.7 5.7 %collective-permute-start.35 = (f32[128,128]{0,1:T(8,128)S(1)}, f32[128,128]{0,1:T(8,128)S(1)}, u32[]{:S(2)}, u32[]{:S(2)}) collective-permute-start(f32[128,128]{0,1:T(8,128)S(1)} %all_gather.7), channel_id=1, source_target_pairs={{0,6},{1,7},{2,0},{3,1},{4,2},{5,3},{6,4},{7,5},{8,14},{9,15},{10,... | collective-permute-start | bytes 196616 | tf_op jit(solution)/shard_map/ppermute | solution.py:15
  163.8 4.7 %collective-permute-start.34 = (f32[128,128]{0,1:T(8,128)S(1)}, f32[128,128]{0,1:T(8,128)S(1)}, u32[]{:S(2)}, u32[]{:S(2)}) collective-permute-start(f32[128,128]{0,1:T(8,128)S(1)} %all_gather.7), channel_id=1, source_target_pairs={{0,7},{1,0},{2,1},{3,2},{4,3},{5,4},{6,5},{7,6},{8,15},{9,8},{10,9... | collective-permute-start | bytes 196616 | tf_op jit(solution)/shard_map/ppermute | solution.py:15
  163.8 4.6 %collective-permute-start.33 = (f32[128,128]{0,1:T(8,128)S(1)}, f32[128,128]{0,1:T(8,128)S(1)}, u32[]{:S(2)}, u32[]{:S(2)}) collective-permute-start(f32[128,128]{0,1:T(8,128)S(1)} %all_gather.7), channel_id=1, source_target_pairs={{0,1},{1,2},{2,3},{3,4},{4,5},{5,6},{6,7},{7,0},{8,9},{9,10},{10,1... | collective-permute-start | bytes 196616 | tf_op jit(solution)/shard_map/ppermute | solution.py:15
  (19 other events, 245.9 us)
where the time goes:
time: 198 us
  waiting for transfers between devices  78.8 us (40%)
  blocking collectives  58.2 us (29%)
  starting transfers between devices  35.7 us (18%)
  local copies, waits for them, and re-layouts  11.4 us (6%)
  other arithmetic  5.05 us (3%)
  matrix products  4.71 us (2%)
  between operations  3.71 us (2%)
    ppermute x4, waiting for transfers between devices, padded_2(): before = lax.ppermute(last, axis, up)  31.3 us
    ppermute x28, waiting for transfers between devices, from_behind(): return lax.ppermute(value, axis, pairs)  30.8 us
    ppermute x28, starting transfers between devices, from_behind(): return lax.ppermute(value, axis, pairs)  24.1 us
    all_to_all x1, blocking collectives, shards(): lax.all_to_all(analysis, 'mem', split_axis=0, concat_axis=2, tiled=True)  19.5 us
    ppermute x4, waiting for transfers between devices, padded_2(): after = lax.ppermute(initial, axis, down)  16.7 us
    all_gather x1, blocking collectives, shards(): weight_rows = lax.all_gather(weight, 'mem', axis=1, tiled=True)  13.8 us
    all_gather x1, blocking collectives, shards(): own_rows = lax.all_gather(observed, 'mem', axis=0, tiled=True)  13.4 us
    pmax x1, blocking collectives, shards(): both = lax.pmax((row_max, -var_min), 'space')  11.5 us
  transfers between devices with their start and end apart: 37, of which 27 were waited for; matrix products, arithmetic and copies ran while one was open for 3% of the time, Pallas kernels for 0%

commit v1 on v0

--- a/solution.py
+++ b/solution.py
@@ -1,3 +1,4 @@
+import functools
 import jax
 import jax.numpy as jnp
 from jax import lax
@@ -7,6 +8,33 @@
 ITERS = 6
 time_step = 0.05
 highest = lax.Precision.HIGHEST
+
+
+def build_row(here_x, k_dim):
+    block_last = list(here_x.shape[1:])
+    block_last[k_dim] *= here_x.shape[0]
+    return jnp.moveaxis(here_x, 0, k_dim).reshape(block_last)
+
+
+def _keep_up_point(block_here, mesh_dim):
+    k_all = lax.axis_size(mesh_dim)
+    piece_next = block_here[None]
+    for b in range(k_all.bit_length() - 1):
+        local_out = 1 << b
+        piece_out = lax.ppermute(
+            piece_next, axis_name=mesh_dim, perm=[(w, w ^ local_out) for w in range(k_all)]
+        )
+        all_rows = jnp.stack([piece_next, piece_out])
+        m_next = lax.axis_index(mesh_dim) >> b & 1
+        piece_next = jnp.where(m_next == 0, all_rows, all_rows[::-1]).reshape(-1, *block_here.shape)
+    return piece_next
+
+
+def balance_pools(row_data, payload, ndim_at):
+    return build_row(_keep_up_point(row_data, payload), ndim_at)
+
+
+recast_thing = functools.partial(balance_pools, payload="mem", ndim_at=1)
 
 
 def from_behind(value, axis, steps):
@@ -124,7 +152,7 @@
             rho_now = rho_next
     weight = anom_weight + mean_weight[:, None]
     owned_cells = lax.all_to_all(states, "mem", split_axis=2, concat_axis=0, tiled=True)
-    weight_rows = lax.all_gather(weight, "mem", axis=1, tiled=True)
+    weight_rows = recast_thing(weight)
     weight_context = collect_band(weight_rows, 0, reach_slabs, move_weights)
     own_plane_ids = space_index * planes_dev + jnp.arange(planes_dev, dtype=jnp.int32)
     plane_taper = taper_of(own_plane_ids, context_planes, planes_all, reach_planes)

time: 198 us -> 190 us (0.960)
  blocking collectives: 58.2 us -> 41.3 us
  waiting for transfers between devices: 78.8 us -> 85.3 us
  starting transfers between devices: 35.7 us -> 38.2 us
    all_gather x1 -> x0, blocking collectives: 13.8 us -> none  [shards(): weight_rows = lax.all_gather(weight, 'mem', axis=1, tiled=True)]
    all_to_all x1, waiting for transfers between devices: 0.01 us -> 4.2 us  [shards(): lax.all_to_all(states, 'mem', split_axis=2, concat_axis=0, tiled=True)]
    ppermute x0 -> x2, starting transfers between devices: none -> 3.38 us  [_keep_up_point(): lax.ppermute(piece_next, axis_name=mesh_dim, perm=[(w, w ^ local_out) for...]
    all_to_all x1, blocking collectives: 19.5 us -> 16.4 us  [shards(): lax.all_to_all(analysis, 'mem', split_axis=0, concat_axis=2, tiled=True)]
    ppermute x0 -> x2, waiting for transfers between devices: none -> 2.3 us  [_keep_up_point(): lax.ppermute(piece_next, axis_name=mesh_dim, perm=[(w, w ^ local_out) for...]
    unnamed x37 -> x35, local copies, waits for them, and re-layouts: 6.2 us -> 6.2 us
  transfers between devices with their start and end apart: 37 -> 39, of which waited for: 27 -> 30; matrix products, arithmetic and copies ran while one was open for 3% -> 3% of each run, Pallas kernels for 0% -> 0%
where the time goes in v1:
time: 190 us
  waiting for transfers between devices  85.3 us (45%)
  blocking collectives  41.3 us (22%)
  starting transfers between devices  38.2 us (20%)
  local copies, waits for them, and re-layouts  11.4 us (6%)
  other arithmetic  5.09 us (3%)
  matrix products  4.7 us (2%)
  between operations  3.78 us (2%)
    ppermute x4, waiting for transfers between devices, padded_2(): before = lax.ppermute(last, axis, up)  31.3 us
    ppermute x28, waiting for transfers between devices, from_behind(): return lax.ppermute(value, axis, pairs)  30.8 us
    ppermute x28, starting transfers between devices, from_behind(): return lax.ppermute(value, axis, pairs)  24.4 us
    ppermute x4, waiting for transfers between devices, padded_2(): after = lax.ppermute(initial, axis, down)  16.7 us
    all_to_all x1, blocking collectives, shards(): lax.all_to_all(analysis, 'mem', split_axis=0, concat_axis=2, tiled=True)  16.4 us
    all_gather x1, blocking collectives, shards(): own_rows = lax.all_gather(observed, 'mem', axis=0, tiled=True)  13.4 us
    pmax x1, blocking collectives, shards(): both = lax.pmax((row_max, -var_min), 'space')  11.5 us
    unnamed x35, local copies, waits for them, and re-layouts  6.2 us
  transfers between devices with their start and end apart: 39, of which 30 were waited for; matrix products, arithmetic and copies ran while one was open for 3% of the time, Pallas kernels for 0%

profile of v1, /device:TPU:6, one launch (start us, length us, event | category | flops | bytes accessed | tf_op | source)
XLA Modules:
  0.0 189.9 jit_solution(15638196966442525447)
XLA Ops:
  1.9 10.0 %collective-permute-done = f32[32,2,2048]{2,0,1:T(8,128)S(1)} collective-permute-done((f32[32,2,2048]{2,0,1:T(8,128)S(1)}, f32[32,2,2048]{2,0,1:T(8,128)S(1)}, u32[]{:S(2)}, u32[]{:S(2)}) %collective-permute-start) | collective-permute-done | bytes 524320 | tf_op jit(solution)/shard_map/ppermute | solution.py:54
  12.0 3.6 %collective-permute-done.1 = f32[32,2,2048]{2,0,1:T(8,128)S(1)} collective-permute-done((f32[32,2,2048]{2,0,1:T(8,128)S(1)}, f32[32,2,2048]{2,0,1:T(8,128)S(1)}, u32[]{:S(2)}, u32[]{:S(2)}) %collective-permute-start.1) | collective-permute-done | bytes 524320 | tf_op jit(solution)/shard_map/ppermute | solution.py:53
  18.3 10.7 %collective-permute-done.3 = f32[32,2,2048]{2,0,1:T(8,128)S(1)} collective-permute-done((f32[32,2,2048]{2,0,1:T(8,128)S(1)}, f32[32,2,2048]{2,0,1:T(8,128)S(1)}, u32[]{:S(2)}, u32[]{:S(2)}) %collective-permute-start.3) | collective-permute-done | bytes 524320 | tf_op jit(solution)/shard_map/ppermute | solution.py:53
  33.4 7.9 %collective-permute-done.5 = f32[32,2,2048]{2,0,1:T(8,128)S(1)} collective-permute-done((f32[32,2,2048]{2,0,1:T(8,128)S(1)}, f32[32,2,2048]{2,0,1:T(8,128)S(1)}, u32[]{:S(2)}, u32[]{:S(2)}) %collective-permute-start.5) | collective-permute-done | bytes 524320 | tf_op jit(solution)/shard_map/ppermute | solution.py:53
  41.4 2.9 %collective-permute-done.4 = f32[32,2,2048]{2,0,1:T(8,128)S(1)} collective-permute-done((f32[32,2,2048]{2,0,1:T(8,128)S(1)}, f32[32,2,2048]{2,0,1:T(8,128)S(1)}, u32[]{:S(2)}, u32[]{:S(2)}) %collective-permute-start.4) | collective-permute-done | bytes 524320 | tf_op jit(solution)/shard_map/ppermute | solution.py:54
  46.8 9.0 %collective-permute-done.7 = f32[32,2,2048]{2,0,1:T(8,128)S(1)} collective-permute-done((f32[32,2,2048]{2,0,1:T(8,128)S(1)}, f32[32,2,2048]{2,0,1:T(8,128)S(1)}, u32[]{:S(2)}, u32[]{:S(2)}) %collective-permute-start.7) | collective-permute-done | bytes 524320 | tf_op jit(solution)/shard_map/ppermute | solution.py:53
  55.7 3.0 %collective-permute-done.6 = f32[32,2,2048]{2,0,1:T(8,128)S(1)} collective-permute-done((f32[32,2,2048]{2,0,1:T(8,128)S(1)}, f32[32,2,2048]{2,0,1:T(8,128)S(1)}, u32[]{:S(2)}, u32[]{:S(2)}) %collective-permute-start.6) | collective-permute-done | bytes 524320 | tf_op jit(solution)/shard_map/ppermute | solution.py:54
  60.1 13.4 %all_gather.3 = f32[128,128]{1,0:T(8,128)S(1)} all-gather(f32[32,128]{1,0:T(8,128)S(1)} %select_bitcast_fusion), channel_id=1, replica_groups=mesh['mem'=4,'space'=8] {'mem'}, dimensions={0}, use_global_device_ids=true | all-gather | bytes 81920 | tf_op jit(solution)/shard_map/all_gather | solution.py:110
  73.6 3.9 %collective-permute-start.8 = (f32[129,128]{1,0:T(8,128)S(1)}, f32[129,128]{1,0:T(8,128)S(1)}, u32[]{:S(2)}, u32[]{:S(2)}) collective-permute-start(f32[129,128]{1,0:T(8,128)S(1)} %pad_maximum_fusion.8), channel_id=1, source_target_pairs={{0,2},{1,3},{2,4},{3,5},{4,6},{5,7},{6,0},{7,1},{8,10},{9,11},{10,... | collective-permute-start | bytes 198152 | tf_op jit(solution)/shard_map/ppermute | solution.py:43
  79.4 2.5 %collective-permute-done.9 = f32[129,128]{1,0:T(8,128)S(1)} collective-permute-done((f32[129,128]{1,0:T(8,128)S(1)}, f32[129,128]{1,0:T(8,128)S(1)}, u32[]{:S(2)}, u32[]{:S(2)}) %collective-permute-start.9) | collective-permute-done | bytes 66080 | tf_op jit(solution)/shard_map/ppermute | solution.py:43
  84.6 11.5 %all-reduce = (f32[]{:T(128)}, f32[]{:T(128)}) all-reduce(f32[]{:T(128)} %reduce_max.9, f32[]{:T(128)S(6)} %neg.6), channel_id=1, replica_groups=mesh['mem'=4,'space'=8] {'space'}, use_global_device_ids=true, to_apply=%region_3.4 | all-reduce | flops 2 | bytes 16 | tf_op jit(solution)/shard_map/pmax | solution.py:124
  97.5 4.1 %collective-permute-start.12 = (f32[128,33]{0,1:T(8,128)S(1)}, f32[128,33]{0,1:T(8,128)S(1)}, u32[]{:S(2)}, u32[]{:S(2)}) collective-permute-start(f32[128,33]{0,1:T(8,128)S(1)} %pad_maximum_fusion.11), channel_id=1, source_target_pairs={{0,2},{1,3},{2,4},{3,5},{4,6},{5,7},{6,0},{7,1},{8,10},{9,11},{10,... | collective-permute-start | bytes 50696 | tf_op jit(solution)/shard_map/ppermute | solution.py:43
  103.0 2.8 %collective-permute-done.13 = f32[128,33]{0,1:T(8,128)S(1)} collective-permute-done((f32[128,33]{0,1:T(8,128)S(1)}, f32[128,33]{0,1:T(8,128)S(1)}, u32[]{:S(2)}, u32[]{:S(2)}) %collective-permute-start.13) | collective-permute-done | bytes 16928 | tf_op jit(solution)/shard_map/ppermute | solution.py:43
  107.7 2.4 %collective-permute-start.16 = (f32[128,33]{0,1:T(8,128)S(1)}, f32[128,33]{0,1:T(8,128)S(1)}, u32[]{:S(2)}, u32[]{:S(2)}) collective-permute-start(f32[128,33]{0,1:T(8,128)S(1)} %pad_maximum_fusion.12), channel_id=1, source_target_pairs={{0,2},{1,3},{2,4},{3,5},{4,6},{5,7},{6,0},{7,1},{8,10},{9,11},{10,... | collective-permute-start | bytes 50696 | tf_op jit(solution)/shard_map/ppermute | solution.py:43
  115.5 2.4 %collective-permute-start.20 = (f32[128,33]{0,1:T(8,128)S(1)}, f32[128,33]{0,1:T(8,128)S(1)}, u32[]{:S(2)}, u32[]{:S(2)}) collective-permute-start(f32[128,33]{0,1:T(8,128)S(1)} %pad_maximum_fusion.13), channel_id=1, source_target_pairs={{0,2},{1,3},{2,4},{3,5},{4,6},{5,7},{6,0},{7,1},{8,10},{9,11},{10,... | collective-permute-start | bytes 50696 | tf_op jit(solution)/shard_map/ppermute | solution.py:43
  123.3 2.4 %collective-permute-start.24 = (f32[128,33]{0,1:T(8,128)S(1)}, f32[128,33]{0,1:T(8,128)S(1)}, u32[]{:S(2)}, u32[]{:S(2)}) collective-permute-start(f32[128,33]{0,1:T(8,128)S(1)} %pad_maximum_fusion.14), channel_id=1, source_target_pairs={{0,2},{1,3},{2,4},{3,5},{4,6},{5,7},{6,0},{7,1},{8,10},{9,11},{10,... | collective-permute-start | bytes 50696 | tf_op jit(solution)/shard_map/ppermute | solution.py:43
  131.2 2.4 %collective-permute-start.28 = (f32[128,33]{0,1:T(8,128)S(1)}, f32[128,33]{0,1:T(8,128)S(1)}, u32[]{:S(2)}, u32[]{:S(2)}) collective-permute-start(f32[128,33]{0,1:T(8,128)S(1)} %pad_maximum_fusion.15), channel_id=1, source_target_pairs={{0,2},{1,3},{2,4},{3,5},{4,6},{5,7},{6,0},{7,1},{8,10},{9,11},{10,... | collective-permute-start | bytes 50696 | tf_op jit(solution)/shard_map/ppermute | solution.py:43
  140.5 2.3 %collective-permute-done.32 = f32[1,128,32]{1,2,0:T(8,128)S(1)} collective-permute-done((f32[1,128,32]{1,2,0:T(8,128)S(1)}, f32[1,128,32]{1,2,0:T(8,128)S(1)}, u32[]{:S(2)}, u32[]{:S(2)}) %collective-permute-start.32) | collective-permute-done | bytes 16416 | tf_op jit(solution)/shard_map/ppermute | solution.py:24
  145.8 2.9 %reshape.51 = f32[4,1,32768]{2,1,0:T(1,128)} reshape(f32[2048,2,32]{2,1,0:T(2,128)S(1)} %bitcast.119) | data formatting | bytes 1048576
  148.6 3.5 %all-to-all-start = ((f32[4,1,32768]{2,1,0:T(1,128)}), f32[4,1,32768]{2,1,0:T(1,128)S(1)}, u32[]{:S(2)}, u32[]{:S(2)}) async-start(f32[4,1,32768]{2,1,0:T(1,128)} %reshape.51), calls=%async_computation | async-start | bytes 1048576 | tf_op jit(solution)/shard_map/all_to_all | solution.py:154
  152.2 2.6 %collective-permute-start.34 = (f32[128,128]{0,1:T(8,128)S(1)}, f32[128,128]{0,1:T(8,128)S(1)}, u32[]{:S(2)}, u32[]{:S(2)}) collective-permute-start(f32[128,128]{0,1:T(8,128)S(1)} %bitcast.124), channel_id=1, source_target_pairs={{0,2},{1,3},{2,4},{3,5},{4,6},{5,7},{6,0},{7,1},{8,10},{9,11},{10,... | collective-permute-start | bytes 196616 | tf_op jit(solution)/shard_map/ppermute | solution.py:43
  156.7 3.0 %collective-permute-done.35 = f32[128,128]{0,1:T(8,128)S(1)} collective-permute-done((f32[128,128]{0,1:T(8,128)S(1)}, f32[128,128]{0,1:T(8,128)S(1)}, u32[]{:S(2)}, u32[]{:S(2)}) %collective-permute-start.35) | collective-permute-done | bytes 65568 | tf_op jit(solution)/shard_map/ppermute | solution.py:43
  161.8 4.2 %all-to-all-done = f32[4,1,32768]{2,1,0:T(1,128)S(1)} async-done(((f32[4,1,32768]{2,1,0:T(1,128)}), f32[4,1,32768]{2,1,0:T(1,128)S(1)}, u32[]{:S(2)}, u32[]{:S(2)}) %all-to-all-start) | async-done | bytes 524320 | tf_op jit(solution)/shard_map/all_to_all | solution.py:154
  172.5 16.4 %all_to_all.36 = f32[128,2,512]{2,1,0:T(2,128)S(1)} all-to-all(f32[128,2,512]{2,1,0:T(2,128)S(1)} %copy.49), channel_id=1, replica_groups=mesh['mem'=4,'space'=8] {'mem'}, dimensions={0} | all-to-all | bytes 1048576 | tf_op jit(solution)/shard_map/all_to_all | solution.py:168
  (171 shorter events, 57.2 us)
Async XLA Ops:
  1.4 10.6 %collective-permute-start = (f32[32,2,2048]{2,0,1:T(8,128)S(1)}, f32[32,2,2048]{2,0,1:T(8,128)S(1)}, u32[]{:S(2)}, u32[]{:S(2)}) collective-permute-start(f32[32,2,2048]{2,0,1:T(8,128)S(1)} %copy.42), channel_id=1, source_target_pairs={{1,0},{2,1},{3,2},{4,3},{5,4},{6,5},{7,6},{0,7},{9,8},{10,9},{11,1... | collective-permute-start | bytes 1572872 | tf_op jit(solution)/shard_map/ppermute | solution.py:54
  1.4 14.2 %collective-permute-start.1 = (f32[32,2,2048]{2,0,1:T(8,128)S(1)}, f32[32,2,2048]{2,0,1:T(8,128)S(1)}, u32[]{:S(2)}, u32[]{:S(2)}) collective-permute-start(f32[32,2,2048]{2,0,1:T(8,128)S(1)} %copy.42), channel_id=1, source_target_pairs={{0,1},{1,2},{2,3},{3,4},{4,5},{5,6},{6,7},{7,0},{8,9},{9,10},{10,1... | collective-permute-start | bytes 1572872 | tf_op jit(solution)/shard_map/ppermute | solution.py:53
  16.5 12.5 %collective-permute-start.3 = (f32[32,2,2048]{2,0,1:T(8,128)S(1)}, f32[32,2,2048]{2,0,1:T(8,128)S(1)}, u32[]{:S(2)}, u32[]{:S(2)}) collective-permute-start(f32[32,2,2048]{2,0,1:T(8,128)S(1)} %fusion.29), channel_id=1, source_target_pairs={{0,1},{1,2},{2,3},{3,4},{4,5},{5,6},{6,7},{7,0},{8,9},{9,10},{10,1... | collective-permute-start | bytes 1572872 | tf_op jit(solution)/shard_map/ppermute | solution.py:53
  16.5 13.3 %collective-permute-start.2 = (f32[32,2,2048]{2,0,1:T(8,128)S(1)}, f32[32,2,2048]{2,0,1:T(8,128)S(1)}, u32[]{:S(2)}, u32[]{:S(2)}) collective-permute-start(f32[32,2,2048]{2,0,1:T(8,128)S(1)} %fusion.29), channel_id=1, source_target_pairs={{1,0},{2,1},{3,2},{4,3},{5,4},{6,5},{7,6},{0,7},{9,8},{10,9},{11,1... | collective-permute-start | bytes 1572872 | tf_op jit(solution)/shard_map/ppermute | solution.py:54
  29.9 11.5 %collective-permute-start.5 = (f32[32,2,2048]{2,0,1:T(8,128)S(1)}, f32[32,2,2048]{2,0,1:T(8,128)S(1)}, u32[]{:S(2)}, u32[]{:S(2)}) collective-permute-start(f32[32,2,2048]{2,0,1:T(8,128)S(1)} %fusion.23), channel_id=1, source_target_pairs={{0,1},{1,2},{2,3},{3,4},{4,5},{5,6},{6,7},{7,0},{8,9},{9,10},{10,1... | collective-permute-start | bytes 1572872 | tf_op jit(solution)/shard_map/ppermute | solution.py:53
  30.0 14.3 %collective-permute-start.4 = (f32[32,2,2048]{2,0,1:T(8,128)S(1)}, f32[32,2,2048]{2,0,1:T(8,128)S(1)}, u32[]{:S(2)}, u32[]{:S(2)}) collective-permute-start(f32[32,2,2048]{2,0,1:T(8,128)S(1)} %fusion.23), channel_id=1, source_target_pairs={{1,0},{2,1},{3,2},{4,3},{5,4},{6,5},{7,6},{0,7},{9,8},{10,9},{11,1... | collective-permute-start | bytes 1572872 | tf_op jit(solution)/shard_map/ppermute | solution.py:54
  44.4 11.3 %collective-permute-start.7 = (f32[32,2,2048]{2,0,1:T(8,128)S(1)}, f32[32,2,2048]{2,0,1:T(8,128)S(1)}, u32[]{:S(2)}, u32[]{:S(2)}) collective-permute-start(f32[32,2,2048]{2,0,1:T(8,128)S(1)} %fusion.17), channel_id=1, source_target_pairs={{0,1},{1,2},{2,3},{3,4},{4,5},{5,6},{6,7},{7,0},{8,9},{9,10},{10,1... | collective-permute-start | bytes 1572872 | tf_op jit(solution)/shard_map/ppermute | solution.py:53
  44.6 14.1 %collective-permute-start.6 = (f32[32,2,2048]{2,0,1:T(8,128)S(1)}, f32[32,2,2048]{2,0,1:T(8,128)S(1)}, u32[]{:S(2)}, u32[]{:S(2)}) collective-permute-start(f32[32,2,2048]{2,0,1:T(8,128)S(1)} %fusion.17), channel_id=1, source_target_pairs={{1,0},{2,1},{3,2},{4,3},{5,4},{6,5},{7,6},{0,7},{9,8},{10,9},{11,1... | collective-permute-start | bytes 1572872 | tf_op jit(solution)/shard_map/ppermute | solution.py:54
  73.6 5.9 %collective-permute-start.8 = (f32[129,128]{1,0:T(8,128)S(1)}, f32[129,128]{1,0:T(8,128)S(1)}, u32[]{:S(2)}, u32[]{:S(2)}) collective-permute-start(f32[129,128]{1,0:T(8,128)S(1)} %pad_maximum_fusion.8), channel_id=1, source_target_pairs={{0,2},{1,3},{2,4},{3,5},{4,6},{5,7},{6,0},{7,1},{8,10},{9,11},{10,... | collective-permute-start | bytes 198152 | tf_op jit(solution)/shard_map/ppermute | solution.py:43
  77.5 5.8 %collective-permute-start.11 = (f32[129,128]{1,0:T(8,128)S(1)}, f32[129,128]{1,0:T(8,128)S(1)}, u32[]{:S(2)}, u32[]{:S(2)}) collective-permute-start(f32[129,128]{1,0:T(8,128)S(1)} %pad_maximum_fusion.8), channel_id=1, source_target_pairs={{0,6},{1,7},{2,0},{3,1},{4,2},{5,3},{6,4},{7,5},{8,14},{9,15},{10,... | collective-permute-start | bytes 198152 | tf_op jit(solution)/shard_map/ppermute | solution.py:43
  77.5 4.4 %collective-permute-start.10 = (f32[129,128]{1,0:T(8,128)S(1)}, f32[129,128]{1,0:T(8,128)S(1)}, u32[]{:S(2)}, u32[]{:S(2)}) collective-permute-start(f32[129,128]{1,0:T(8,128)S(1)} %pad_maximum_fusion.8), channel_id=1, source_target_pairs={{0,7},{1,0},{2,1},{3,2},{4,3},{5,4},{6,5},{7,6},{8,15},{9,8},{10,9... | collective-permute-start | bytes 198152 | tf_op jit(solution)/shard_map/ppermute | solution.py:43
  77.5 4.4 %collective-permute-start.9 = (f32[129,128]{1,0:T(8,128)S(1)}, f32[129,128]{1,0:T(8,128)S(1)}, u32[]{:S(2)}, u32[]{:S(2)}) collective-permute-start(f32[129,128]{1,0:T(8,128)S(1)} %pad_maximum_fusion.8), channel_id=1, source_target_pairs={{0,1},{1,2},{2,3},{3,4},{4,5},{5,6},{6,7},{7,0},{8,9},{9,10},{10,1... | collective-permute-start | bytes 198152 | tf_op jit(solution)/shard_map/ppermute | solution.py:43
  97.5 5.6 %collective-permute-start.12 = (f32[128,33]{0,1:T(8,128)S(1)}, f32[128,33]{0,1:T(8,128)S(1)}, u32[]{:S(2)}, u32[]{:S(2)}) collective-permute-start(f32[128,33]{0,1:T(8,128)S(1)} %pad_maximum_fusion.11), channel_id=1, source_target_pairs={{0,2},{1,3},{2,4},{3,5},{4,6},{5,7},{6,0},{7,1},{8,10},{9,11},{10,... | collective-permute-start | bytes 50696 | tf_op jit(solution)/shard_map/ppermute | solution.py:43
  102.3 4.8 %collective-permute-start.15 = (f32[128,33]{0,1:T(8,128)S(1)}, f32[128,33]{0,1:T(8,128)S(1)}, u32[]{:S(2)}, u32[]{:S(2)}) collective-permute-start(f32[128,33]{0,1:T(8,128)S(1)} %pad_maximum_fusion.11), channel_id=1, source_target_pairs={{0,6},{1,7},{2,0},{3,1},{4,2},{5,3},{6,4},{7,5},{8,14},{9,15},{10,... | collective-permute-start | bytes 50696 | tf_op jit(solution)/shard_map/ppermute | solution.py:43
  110.2 4.8 %collective-permute-start.19 = (f32[128,33]{0,1:T(8,128)S(1)}, f32[128,33]{0,1:T(8,128)S(1)}, u32[]{:S(2)}, u32[]{:S(2)}) collective-permute-start(f32[128,33]{0,1:T(8,128)S(1)} %pad_maximum_fusion.12), channel_id=1, source_target_pairs={{0,6},{1,7},{2,0},{3,1},{4,2},{5,3},{6,4},{7,5},{8,14},{9,15},{10,... | collective-permute-start | bytes 50696 | tf_op jit(solution)/shard_map/ppermute | solution.py:43
  118.0 4.8 %collective-permute-start.23 = (f32[128,33]{0,1:T(8,128)S(1)}, f32[128,33]{0,1:T(8,128)S(1)}, u32[]{:S(2)}, u32[]{:S(2)}) collective-permute-start(f32[128,33]{0,1:T(8,128)S(1)} %pad_maximum_fusion.13), channel_id=1, source_target_pairs={{0,6},{1,7},{2,0},{3,1},{4,2},{5,3},{6,4},{7,5},{8,14},{9,15},{10,... | collective-permute-start | bytes 50696 | tf_op jit(solution)/shard_map/ppermute | solution.py:43
  125.8 4.8 %collective-permute-start.27 = (f32[128,33]{0,1:T(8,128)S(1)}, f32[128,33]{0,1:T(8,128)S(1)}, u32[]{:S(2)}, u32[]{:S(2)}) collective-permute-start(f32[128,33]{0,1:T(8,128)S(1)} %pad_maximum_fusion.14), channel_id=1, source_target_pairs={{0,6},{1,7},{2,0},{3,1},{4,2},{5,3},{6,4},{7,5},{8,14},{9,15},{10,... | collective-permute-start | bytes 50696 | tf_op jit(solution)/shard_map/ppermute | solution.py:43
  133.7 4.8 %collective-permute-start.31 = (f32[128,33]{0,1:T(8,128)S(1)}, f32[128,33]{0,1:T(8,128)S(1)}, u32[]{:S(2)}, u32[]{:S(2)}) collective-permute-start(f32[128,33]{0,1:T(8,128)S(1)} %pad_maximum_fusion.15), channel_id=1, source_target_pairs={{0,6},{1,7},{2,0},{3,1},{4,2},{5,3},{6,4},{7,5},{8,14},{9,15},{10,... | collective-permute-start | bytes 50696 | tf_op jit(solution)/shard_map/ppermute | solution.py:43
  142.8 9.3 %collective-permute-start.33 = (f32[2,128,32]{1,2,0:T(8,128)S(1)}, f32[2,128,32]{1,2,0:T(8,128)S(1)}, u32[]{:S(2)}, u32[]{:S(2)}) collective-permute-start(f32[2,128,32]{1,2,0:T(8,128)S(1)} %get-tuple-element.71), channel_id=1, source_target_pairs={{0,16},{8,24},{16,0},{24,8},{1,17},{9,25},{17,1},{25,9},{2,18},{10... | collective-permute-start | bytes 98312 | tf_op jit(solution)/shard_map/ppermute | solution.py:24
  148.6 17.4 %all-to-all-start = ((f32[4,1,32768]{2,1,0:T(1,128)}), f32[4,1,32768]{2,1,0:T(1,128)S(1)}, u32[]{:S(2)}, u32[]{:S(2)}) async-start(f32[4,1,32768]{2,1,0:T(1,128)} %reshape.51), calls=%async_computation | async-start | bytes 1048576 | tf_op jit(solution)/shard_map/all_to_all | solution.py:154
  152.2 4.5 %collective-permute-start.34 = (f32[128,128]{0,1:T(8,128)S(1)}, f32[128,128]{0,1:T(8,128)S(1)}, u32[]{:S(2)}, u32[]{:S(2)}) collective-permute-start(f32[128,128]{0,1:T(8,128)S(1)} %bitcast.124), channel_id=1, source_target_pairs={{0,2},{1,3},{2,4},{3,5},{4,6},{5,7},{6,0},{7,1},{8,10},{9,11},{10,... | collective-permute-start | bytes 196616 | tf_op jit(solution)/shard_map/ppermute | solution.py:43
  154.9 5.7 %collective-permute-start.37 = (f32[128,128]{0,1:T(8,128)S(1)}, f32[128,128]{0,1:T(8,128)S(1)}, u32[]{:S(2)}, u32[]{:S(2)}) collective-permute-start(f32[128,128]{0,1:T(8,128)S(1)} %bitcast.125), channel_id=1, source_target_pairs={{0,6},{1,7},{2,0},{3,1},{4,2},{5,3},{6,4},{7,5},{8,14},{9,15},{10,... | collective-permute-start | bytes 196616 | tf_op jit(solution)/shard_map/ppermute | solution.py:43
  154.9 4.7 %collective-permute-start.36 = (f32[128,128]{0,1:T(8,128)S(1)}, f32[128,128]{0,1:T(8,128)S(1)}, u32[]{:S(2)}, u32[]{:S(2)}) collective-permute-start(f32[128,128]{0,1:T(8,128)S(1)} %bitcast.126), channel_id=1, source_target_pairs={{0,7},{1,0},{2,1},{3,2},{4,3},{5,4},{6,5},{7,6},{8,15},{9,8},{10,9... | collective-permute-start | bytes 196616 | tf_op jit(solution)/shard_map/ppermute | solution.py:43
  155.0 4.6 %collective-permute-start.35 = (f32[128,128]{0,1:T(8,128)S(1)}, f32[128,128]{0,1:T(8,128)S(1)}, u32[]{:S(2)}, u32[]{:S(2)}) collective-permute-start(f32[128,128]{0,1:T(8,128)S(1)} %bitcast.127), channel_id=1, source_target_pairs={{0,1},{1,2},{2,3},{3,4},{4,5},{5,6},{6,7},{7,0},{8,9},{9,10},{10,1... | collective-permute-start | bytes 196616 | tf_op jit(solution)/shard_map/ppermute | solution.py:43
  (20 other events, 221.5 us)
